TPU v7x, 32 devices: a whole 2x2x4 slice. The times are simulated.
32 devices in a mesh: group: 2 (over y), inner: 4 (over z), outer: 2 (over x), cuts: 2 (over core).
Axes of the slice: x: 2, y: 2, z: 4, core: 2. Of those that a mesh axis runs over, the one named last changes fastest.
Arguments:
- volume: bfloat16 [96, 128, 256], P(('group', 'inner', 'outer'), None, 'cuts'), parts along dimension 0, may hold values from -6 to 6
- projector: bfloat16 [256, 4, 128, 128], P(('inner', 'outer')), may hold values from 0.19921875 to 1
- slot_ray: int32 [256], P(('inner', 'outer')), may hold values from 0 to 63, as said below
- slot_pixel: int32 [256, 4], P(('inner', 'outer')), may hold values from 0 to 5, as said below
- sinogram: bfloat16 [128, 128, 256], P(('group', 'inner', 'outer'), None, 'cuts'), parts along dimension 0, may hold values from -240 to 240
- weight_index: int32 [128, 128], P(('group', 'inner', 'outer')), parts along dimension 0, may hold values from 0 to 15
- weight_table: bfloat16 [16], replicated, may hold values from 0.099609375 to 1
Outputs:
- updated: float32 [96, 128, 256], P(('group', 'inner', 'outer'), None, 'cuts'), parts along dimension 0
There are 2 independent parts, one for each index of `group`. A program takes and returns all parts, laid end to end along the dimension named above; an argument that names none is the same for every part. Nothing has to cross between parts.
Inputs may be any that keep to these rules, and one draw needn't show every extreme that they name: `slot_ray`: each patch lists 32 ray tiles, possibly some more than once. At most 16 of one patch's slots name ray tiles of one band k * 16 to (k + 1) * 16 - 1, and in every draw some band receives exactly 16 slots from every patch. `slot_pixel`: the 4 entries of a slot are different pixel tiles of its own patch; every pixel tile of a patch is named by some slot of that patch.
All inputs are finite; a program needn't handle non-finite values.
Results may differ from a plain program's by a relative error of at most 0.0003.
Values may be sent and summed in bfloat16 or wider, within the bound.
A program may use at most 64 MiB of HBM per device.

v0:
```python
import jax
import jax.numpy as jnp
from jax import lax
from jax.sharding import PartitionSpec as P


def on_device(volume, projector, slot_ray, slot_pixel, sinogram, weight_index, weight_table):
    inners = lax.axis_size("inner")
    outers = lax.axis_size("outer")
    slot_count = projector.shape[0]
    per_slot = projector.shape[1]
    tile_rows = projector.shape[2]
    tile_cols = projector.shape[3]
    patch_tiles = volume.shape[0]
    slice_count = volume.shape[2]
    owned_rows = sinogram.shape[0]
    band_rows = owned_rows * outers
    capacity = 2 * slot_count // inners
    cell_count = inners * capacity
    target = slot_ray // band_rows
    offset = slot_ray % band_rows
    same_target = target[:, None] == target[None, :]
    earlier = jnp.arange(slot_count)[:, None] > jnp.arange(slot_count)[None, :]
    slot_rank = jnp.sum(jnp.logical_and(same_target, earlier), axis=1)
    position = target * capacity + slot_rank
    partial_value = jnp.zeros((slot_count, tile_rows, slice_count), jnp.float32)
    for column in range(per_slot):
        pixels = volume[slot_pixel[:, column]]
        partial_value = partial_value + jnp.einsum(
            "srp,spc->src", projector[:, column], pixels, preferred_element_type=jnp.float32
        )
    outgoing = (
        jnp.zeros((cell_count, tile_rows, slice_count), jnp.float32).at[position].set(partial_value)
    )
    labels = jnp.full((cell_count,), -1.0, jnp.float32).at[position].set(offset.astype(jnp.float32))
    arrived, arrived_rows = (
        lax.all_to_all(
            outgoing.reshape(inners, capacity, tile_rows, slice_count),
            "inner",
            split_axis=0,
            concat_axis=0,
            tiled=True,
        ),
        lax.all_to_all(
            labels.reshape(inners, capacity), "inner", split_axis=0, concat_axis=0, tiled=True
        ),
    )
    selector = (
        jnp.arange(band_rows, dtype=jnp.float32)[:, None] == arrived_rows.reshape(1, cell_count)
    ).astype(jnp.float32)
    block_sums = jnp.dot(
        selector,
        arrived.reshape(cell_count, tile_rows * slice_count),
        precision=lax.Precision.HIGHEST,
    ).reshape(band_rows, tile_rows, slice_count)
    classes = weight_table.shape[0]
    lookup = weight_index[:, :, None] == jnp.arange(classes)[None, None, :]
    weights = jnp.sum(
        jnp.where(lookup, weight_table[None, None, :], jnp.zeros((), weight_table.dtype)), axis=2
    )
    own_sums = lax.psum_scatter(block_sums, "outer", scatter_dimension=0, tiled=True)
    own_residual = (
        weights.astype(jnp.float32)[:, :, None] * (sinogram.astype(jnp.float32) - own_sums)
    ).astype(jnp.bfloat16)
    residual = lax.all_gather(own_residual, "outer", axis=0, tiled=True)
    picked = jnp.dot(
        selector.T.astype(jnp.bfloat16),
        residual.reshape(band_rows, tile_rows * slice_count),
        preferred_element_type=jnp.float32,
    ).astype(jnp.bfloat16)
    returned = lax.all_to_all(
        picked.reshape(inners, capacity, tile_rows, slice_count),
        "inner",
        split_axis=0,
        concat_axis=0,
        tiled=True,
    )
    slot_residual = returned.reshape(cell_count, tile_rows, slice_count)[position]
    owners = jnp.arange(patch_tiles)
    backward = jnp.zeros((patch_tiles, tile_cols, slice_count), jnp.float32)
    column_sum = jnp.zeros((patch_tiles, tile_cols), jnp.float32)
    for column in range(per_slot):
        member = (owners[:, None] == slot_pixel[None, :, column]).astype(jnp.float32)
        spread = jnp.einsum(
            "srp,src->spc", projector[:, column], slot_residual, preferred_element_type=jnp.float32
        )
        backward = backward + jnp.einsum(
            "ts,spc->tpc", member, spread, precision=lax.Precision.HIGHEST
        )
        column_sum = column_sum + jnp.dot(
            member,
            jnp.sum(projector[:, column], axis=1, dtype=jnp.float32),
            precision=lax.Precision.HIGHEST,
        )
    return volume.astype(jnp.float32) + backward / column_sum[:, :, None]


def solution(mesh):
    in_specs = (
        P(("group", "inner", "outer"), None, "cuts"),
        P(("inner", "outer"), None, None, None),
        P(("inner", "outer")),
        P(("inner", "outer"), None),
        P(("group", "inner", "outer"), None, "cuts"),
        P(("group", "inner", "outer"), None),
        P(),
    )
    out_specs = P(("group", "inner", "outer"), None, "cuts")
    return jax.shard_map(
        on_device, mesh=mesh, in_specs=in_specs, out_specs=out_specs, check_vma=False
    )
```

profile of v0, /device:TPU:0, one launch (start us, length us, event | category | flops | bytes accessed | tf_op | source)
XLA Modules:
  0.0 267.4 jit_solution(11891685682074695904)
XLA Ops:
  8.8 6.3 %all-to-all-start = ((f32[4,1,16]{2,1,0:T(1,128)}), f32[4,1,16]{2,1,0:T(1,128)S(1)}, u32[]{:S(2)}, u32[]{:S(2)}) async-start(f32[4,1,16]{2,1,0:T(1,128)} %bitcast.2), calls=%async_computation | async-start | bytes 4096 | tf_op jit(solution)/shard_map/all_to_all | solution.py:44
  19.3 2.2 fusion.12
  21.5 3.4 %fusion.15 = f32[32,128,128]{2,1,0:T(8,128)} fusion(bf16[32,128,128]{2,1,0:T(8,128)(2,1)S(1)} %copy-done.3, bf16[32,4,128,128]{3,2,1,0:T(8,128)(2,1)} %param.8), kind=kOutput, calls=%fused_computation.39 | convolution fusion | flops 134217728 | bytes 4194304 | tf_op jit(solution)/shard_map/srp,spc->src/dot_general | solution.py:29
  25.7 3.5 %fusion.9 = f32[32,128,128]{2,1,0:T(8,128)} fusion(bf16[32,128,128]{2,1,0:T(8,128)(2,1)S(1)} %gather_fusion.2, bf16[32,4,128,128]{3,2,1,0:T(8,128)(2,1)} %param.8), kind=kOutput, calls=%fused_computation.33 | convolution fusion | flops 134217728 | bytes 4194304 | tf_op jit(solution)/shard_map/srp,spc->src/dot_general | solution.py:29
  29.9 4.8 %add_bitcast_fusion = f32[32,128,128]{1,2,0:T(8,128)} fusion(f32[32,128,128]{2,1,0:T(8,128)} %fusion.9, f32[32,128,128]{2,1,0:T(8,128)} %fusion.15, f32[32,128,128]{2,1,0:T(8,128)S(1)} %fusion.12, bf16[32,128,128]{2,1,0:T(8,128)(2,1)S(1)} %gather_fusion.3, bf16[32,4,128,128]{3,2,1,0:T(8,128)(2,1)} %param.8), kind=kOutput, calls=%fused_computation.16 | convolution fusion | flops 135790592 | bytes 10485760 | tf_op jit(solution)/shard_map/srp,spc->src/dot_general | solution.py:29
  34.7 1.9 copy.92
  36.7 2.4 broadcast_in_dim.18
  39.1 5.4 %scatter_fusion = f32[64,128,128]{2,1,0:T(8,128)} fusion(f32[64,128,128]{2,1,0:T(8,128)} %broadcast_in_dim.18, s32[32]{0:T(128)S(1)} %compare_select_fusion.4, f32[32,128,128]{2,1,0:T(8,128)S(1)} %copy.92), kind=kCustom, calls=%fused_computation.6 | custom fusion | bytes 6291584 | tf_op jit(solution)/shard_map/scatter | solution.py:33
  44.5 5.1 %all-to-all-start.1 = ((f32[4,16,128,128]{3,2,1,0:T(8,128)}), f32[4,16,128,128]{3,2,1,0:T(8,128)}, u32[]{:S(2)}, u32[]{:S(2)}) async-start(f32[4,16,128,128]{3,2,1,0:T(8,128)} %bitcast.117), calls=%async_computation.1 | async-start | bytes 8388608 | tf_op jit(solution)/shard_map/all_to_all | solution.py:37
  50.9 91.7 %all-to-all-done.1 = f32[4,16,128,128]{3,2,1,0:T(8,128)} async-done(((f32[4,16,128,128]{3,2,1,0:T(8,128)}), f32[4,16,128,128]{3,2,1,0:T(8,128)}, u32[]{:S(2)}, u32[]{:S(2)}) %all-to-all-start.1) | async-done | bytes 4194336 | tf_op jit(solution)/shard_map/all_to_all | solution.py:37
  142.6 6.8 %fusion = f32[16,128,128]{2,0,1:T(8,128)} fusion(f32[64]{0:T(128)S(1)} %eq.118, f32[8,8,128,128]{3,2,1,0:T(8,128)} %bitcast.39), kind=kOutput, calls=%fused_computation.9 | convolution fusion | flops 201327616 | bytes 5243136 | tf_op jit(solution)/shard_map/dot_general | solution.py:51
  149.7 19.4 %reduce-scatter.2.cloned.1.call-done = f32[8,128,128]{2,0,1:T(8,128)} async-done(((f32[16,128,128]{2,0,1:T(8,128)}), f32[8,128,128]{2,0,1:T(8,128)}) %reduce-scatter.2.cloned.1.call-update) | async-done | bytes 524304 | tf_op jit(solution)/shard_map/reduce_scatter | solution.py:61
  170.4 8.6 %all_gather.3 = bf16[16,128,128]{2,0,1:T(8,128)(2,1)S(1)} all-gather(bf16[8,128,128]{2,0,1:T(8,128)(2,1)S(1)} %multiply_convert_fusion), channel_id=1, replica_groups=mesh['group'=2,'inner'=4,'outer'=2,'cuts'=2] {'outer'}, dimensions={0}, use_global_device_ids=true | all-gather | bytes 786432 | tf_op jit(solution)/shard_map/all_gather | solution.py:65
  179.7 1.9 copy.120
  181.6 4.6 %all-to-all-start.2 = ((bf16[4,16,128,128]{3,2,1,0:T(8,128)(2,1)}), bf16[4,16,128,128]{3,2,1,0:T(8,128)(2,1)S(1)}, u32[]{:S(2)}, u32[]{:S(2)}) async-start(bf16[4,16,128,128]{3,2,1,0:T(8,128)(2,1)} %bitcast.43), calls=%async_computation.3 | async-start | bytes 4194304 | tf_op jit(solution)/shard_map/all_to_all | solution.py:71
  186.2 3.4 %convert_reduce_fusion = (f32[32,128]{1,0:T(8,128)S(1)}, f32[32,128]{1,0:T(8,128)S(1)}, f32[32,128]{1,0:T(8,128)S(1)}, f32[32,128]{1,0:T(8,128)S(1)}) fusion(bf16[32,4,128,128]{3,2,1,0:T(8,128)(2,1)} %param.8), kind=kLoop, calls=%fused_computation.12 | loop fusion | flops 4177920 | bytes 4259840 | tf_op jit(solution)/shard_map/reduce_sum | solution.py:92
  190.3 43.1 %all-to-all-done.2 = bf16[4,16,128,128]{3,2,1,0:T(8,128)(2,1)S(1)} async-done(((bf16[4,16,128,128]{3,2,1,0:T(8,128)(2,1)}), bf16[4,16,128,128]{3,2,1,0:T(8,128)(2,1)S(1)}, u32[]{:S(2)}, u32[]{:S(2)}) %all-to-all-start.2) | async-done | bytes 2097184 | tf_op jit(solution)/shard_map/all_to_all | solution.py:71
  234.2 3.2 %convolution_bitcast_fusion.3 = f32[32,128,128]{1,2,0:T(8,128)} fusion(bf16[32,128,128]{2,1,0:T(8,128)(2,1)S(1)} %gather_fusion.4, bf16[32,4,128,128]{3,2,1,0:T(8,128)(2,1)} %param.8), kind=kOutput, calls=%fused_computation.20 | convolution fusion | flops 134217728 | bytes 4194304 | tf_op jit(solution)/shard_map/srp,src->spc/dot_general | solution.py:84
  241.7 3.1 %copy.96 = f32[32,128,128]{2,0,1:T(8,128)} copy(f32[32,128,128]{1,2,0:T(8,128)} %convolution_bitcast_fusion.3) | data formatting | bytes 4194304 | tf_op jit(solution)/shard_map/srp,src->spc/dot_general | solution.py:84
  244.7 3.1 %fusion.39 = f32[6,128,128]{2,0,1:T(8,128)} fusion(f32[32,128,128]{2,0,1:T(8,128)} %copy.96, s32[32]{0:T(128)S(1)} %get-tuple-element.15), kind=kOutput, calls=%fused_computation.78 | convolution fusion | flops 37748928 | bytes 2490496 | tf_op jit(solution)/shard_map/ts,spc->tpc/dot_general | solution.py:87
  247.9 3.1 %copy.98 = f32[32,128,128]{2,0,1:T(8,128)} copy(f32[32,128,128]{1,2,0:T(8,128)} %convolution_bitcast_fusion.2) | data formatting | bytes 4194304 | tf_op jit(solution)/shard_map/srp,src->spc/dot_general | solution.py:84
  251.0 2.0 copy.100
  253.1 2.4 copy.102
  255.5 2.5 convolution_add_fusion.2
  (51 shorter events, 19.6 us)
Async XLA Ops:
  6.5 11.1 %copy-start = (bf16[6,128,128]{2,1,0:T(8,128)(2,1)S(1)}, bf16[6,128,128]{2,1,0:T(8,128)(2,1)}, u32[]{:S(2)}) copy-start(bf16[6,128,128]{2,1,0:T(8,128)(2,1)} %param.7) | copy-start | bytes 589828
  8.8 35.7 %all-to-all-start = ((f32[4,1,16]{2,1,0:T(1,128)}), f32[4,1,16]{2,1,0:T(1,128)S(1)}, u32[]{:S(2)}, u32[]{:S(2)}) async-start(f32[4,1,16]{2,1,0:T(1,128)} %bitcast.2), calls=%async_computation | async-start | bytes 4096 | tf_op jit(solution)/shard_map/all_to_all | solution.py:44
  19.3 2.2 copy-start.3
  44.5 98.1 %all-to-all-start.1 = ((f32[4,16,128,128]{3,2,1,0:T(8,128)}), f32[4,16,128,128]{3,2,1,0:T(8,128)}, u32[]{:S(2)}, u32[]{:S(2)}) async-start(f32[4,16,128,128]{3,2,1,0:T(8,128)} %bitcast.117), calls=%async_computation.1 | async-start | bytes 8388608 | tf_op jit(solution)/shard_map/all_to_all | solution.py:37
  49.6 119.5 %reduce-scatter.2.cloned.1.call-start = ((), (), s32[]{:S(2)}) async-start(), calls=%async_computation.4 | async-start | bytes 1572864 | tf_op jit(solution)/shard_map/reduce_scatter | solution.py:61
  142.6 6.9 %copy-start.6 = (s32[8,128]{1,0:T(8,128)S(1)}, s32[8,128]{1,0:T(8,128)}, u32[]{:S(2)}) copy-start(s32[8,128]{1,0:T(8,128)} %param.12) | copy-start | bytes 12292
  142.6 6.9 %copy-start.7 = (bf16[16]{0:T(256)(128)(2,1)S(1)}, bf16[16]{0:T(256)(128)(2,1)}, u32[]{:S(2)}) copy-start(bf16[16]{0:T(256)(128)(2,1)} %param.13) | copy-start | bytes 100
  142.6 26.5 %copy-start.5 = (bf16[8,128,128]{2,1,0:T(8,128)(2,1)S(1)}, bf16[8,128,128]{2,1,0:T(8,128)(2,1)}, u32[]{:S(2)}) copy-start(bf16[8,128,128]{2,1,0:T(8,128)(2,1)} %param.11) | copy-start | bytes 786436
  181.6 51.8 %all-to-all-start.2 = ((bf16[4,16,128,128]{3,2,1,0:T(8,128)(2,1)}), bf16[4,16,128,128]{3,2,1,0:T(8,128)(2,1)S(1)}, u32[]{:S(2)}, u32[]{:S(2)}) async-start(bf16[4,16,128,128]{3,2,1,0:T(8,128)(2,1)} %bitcast.43), calls=%async_computation.3 | async-start | bytes 4194304 | tf_op jit(solution)/shard_map/all_to_all | solution.py:71
  234.2 3.2 %copy-start.1 = (bf16[32,4,128,128]{3,2,1,0:T(8,128)(2,1)S(1)}, bf16[32,4,128,128]{3,2,1,0:T(8,128)(2,1)}, u32[]{:S(2)}) copy-start(bf16[32,4,128,128]{3,2,1,0:T(8,128)(2,1)} %param.8) | copy-start | bytes 12582916
  253.1 2.4 copy-start.4
  255.5 2.5 copy-start.2
Sparse Core Ops, SparseCore 0:
  149.6 19.4 reduce-scatter.1
where the time goes:
time: 268 us; the launch traced here: 267 us
  waiting for transfers between devices  154 us (57%)
  matrix products  36.8 us (14%)
  local copies, waits for them, and re-layouts  31 us (12%)
  starting transfers between devices  16.1 us (6%)
  between operations  13.6 us (5%)
  blocking collectives  8.58 us (3%)
  other arithmetic  7.14 us (3%)
    all_to_all x1, waiting for transfers between devices, on_device(): lax.all_to_all(outgoing.reshape(inners, capacity, tile_rows, slice_count)...  91.7 us
    all_to_all x1, waiting for transfers between devices, on_device(): lax.all_to_all(picked.reshape(inners, capacity, tile_rows, slice_count),...  43.1 us
    reduce_scatter x1, waiting for transfers between devices, on_device(): lax.psum_scatter(block_sums, 'outer', scatter_dimension=0, tiled=True)  19.4 us
    dot_general x4, matrix products, on_device(): jnp.einsum('srp,spc->src', projector[:, column], pixels, preferred_elemen...  13.9 us
    dot_general x4, local copies, waits for them, and re-layouts, on_device(): jnp.einsum('srp,src->spc', projector[:, column], slot_residual, preferred...  10.7 us
    all_gather x1, blocking collectives, on_device(): residual = lax.all_gather(own_residual, 'outer', axis=0, tiled=True)  8.58 us
    dot_general x4, matrix products, on_device(): jnp.einsum('srp,src->spc', projector[:, column], slot_residual, preferred...  7.47 us
    dot_general x4, matrix products, on_device(): jnp.einsum('ts,spc->tpc', member, spread, precision=lax.Precision.HIGHEST)  7.36 us
  transfers between devices with their start and end apart: 4, of which 3 were waited for; matrix products, arithmetic and copies ran while one was open for 13% of the time, Pallas kernels for 0%

commit v1 on v0

--- a/solution.py
+++ b/solution.py
@@ -1,10 +1,17 @@
+import functools
+
 import jax
 import jax.numpy as jnp
 from jax import lax
+from jax.experimental import pallas as pl
+from jax.experimental.pallas import tpu as pltpu
 from jax.sharding import PartitionSpec as P
 
-
-def on_device(volume, projector, slot_ray, slot_pixel, sinogram, weight_index, weight_table):
+MESH = pl.DeviceIdType.MESH
+PIECE = 16
+
+
+def general_path(volume, projector, slot_ray, slot_pixel, sinogram, weight_index, weight_table):
     inners = lax.axis_size("inner")
     outers = lax.axis_size("outer")
     slot_count = projector.shape[0]
@@ -95,6 +102,385 @@
     return volume.astype(jnp.float32) + backward / column_sum[:, :, None]
 
 
+def forward_kernel(first_ref, pixel_ref, volume_ref, projector_ref, packed_ref):
+    step = pl.program_id(0)
+    block, per_slot = projector_ref.shape[:2]
+
+    @pl.when(step == 0)
+    def _():
+        packed_ref[...] = jnp.zeros_like(packed_ref)
+
+    for j in range(block):
+        s = step * block + j
+        pixels = jnp.concatenate(
+            [volume_ref[pixel_ref[s * per_slot + g]] for g in range(per_slot)], axis=0
+        )
+        tiles = jnp.concatenate([projector_ref[j, g] for g in range(per_slot)], axis=1)
+        packed_ref[first_ref[s]] += jnp.dot(tiles, pixels, preferred_element_type=jnp.float32)
+
+
+def backward_kernel(pixel_ref, volume_ref, projector_ref, residual_ref, out_ref, acc_ref):
+    step = pl.program_id(0)
+    block, per_slot, rows, cols = projector_ref.shape
+    slices = residual_ref.shape[-1]
+
+    @pl.when(step == 0)
+    def _():
+        acc_ref[...] = jnp.zeros_like(acc_ref)
+
+    ones = jnp.ones((rows, slices), jnp.bfloat16)
+    for j in range(block):
+        s = step * block + j
+        wide = jnp.concatenate([residual_ref[j], ones], axis=1)
+        tiles = jnp.concatenate([projector_ref[j, g] for g in range(per_slot)], axis=1)
+        spread = lax.dot_general(
+            tiles, wide, (((0,), (0,)), ((), ())), preferred_element_type=jnp.float32
+        )
+        for g in range(per_slot):
+            acc_ref[pixel_ref[s * per_slot + g]] += spread[g * cols : (g + 1) * cols]
+
+    @pl.when(step == pl.num_programs(0) - 1)
+    def _():
+        out_ref[...] = (
+            volume_ref[...].astype(jnp.float32) + acc_ref[:, :, :slices] / acc_ref[:, :, slices:]
+        )
+
+
+def exchange_kernel(n, pieces, own_idx, mate_idx, packed, sino, wts, out_ref, *scratch):
+    take = iter(scratch)
+    mate_part = [next(take) for _ in range(pieces)]
+    from_left, from_right, going, total = (next(take) for _ in range(4))
+    band_res = [next(take) for _ in range(pieces)]
+    picked = [next(take) for _ in range(pieces)]
+    landed = [next(take) for _ in range(pieces)]
+    mate_sino, mate_wts = next(take), next(take)
+    x_send, x_recv, aux_send, aux_recv, sum_send, left_recv, right_recv = (
+        next(take) for _ in range(7)
+    )
+    out_right, out_left, res_recv, pick_send, pick_recv = (next(take) for _ in range(5))
+
+    slots, rows, slices = out_ref.shape
+    owned = sino.shape[0]
+    band = 2 * owned
+    half = rows // 2
+    depth = half // pieces
+    i = lax.axis_index("inner")
+    o = lax.axis_index("outer")
+    mate = {"outer": 1 - o}
+    right = {"inner": i + 1}
+    left = {"inner": i - 1}
+
+    def send(src, dst, ssem, rsem, device):
+        return pltpu.make_async_remote_copy(
+            src_ref=src, dst_ref=dst, send_sem=ssem, recv_sem=rsem, device_id=device,
+            device_id_type=MESH,
+        )
+
+    barrier = pltpu.get_barrier_semaphore()
+    pl.semaphore_signal(barrier, inc=1, device_id=mate, device_id_type=MESH)
+
+    @pl.when(i > 0)
+    def _():
+        pl.semaphore_signal(barrier, inc=1, device_id=left, device_id_type=MESH)
+
+    @pl.when(i < n - 1)
+    def _():
+        pl.semaphore_signal(barrier, inc=1, device_id=right, device_id_type=MESH)
+
+    pl.semaphore_wait(barrier, jnp.where(i > 0, 2, 1) + jnp.where(i < n - 1, 1, 0))
+
+    def mine(c):
+        return pl.ds(pl.multiple_of(o * half + c * depth, depth), depth)
+
+    def theirs(c):
+        return pl.ds(pl.multiple_of((1 - o) * half + c * depth, depth), depth)
+
+    def swap(c):
+        return send(
+            packed.at[pl.ds(0, slots), theirs(c)],
+            mate_part[c].at[pl.ds(0, slots)],
+            x_send.at[c],
+            x_recv.at[c],
+            mate,
+        )
+
+    other_half = pl.ds(pl.multiple_of((1 - o) * half, half), half)
+    aux = [
+        send(sino.at[:, other_half], mate_sino, aux_send.at[0], aux_recv.at[0], mate),
+        send(wts.at[other_half], mate_wts, aux_send.at[1], aux_recv.at[1], mate),
+    ]
+    for c in range(pieces):
+        swap(c).start()
+        if c == min(1, pieces - 1):
+            for copy in aux:
+                copy.start()
+    for c in range(pieces):
+        mate_part[c][slots] = jnp.zeros((depth, slices), jnp.float32)
+
+    def local(c, r):
+        return packed[own_idx[slots + r], mine(c), :] + mate_part[c][mate_idx[slots + r]]
+
+    def loop(count, body):
+        def step(t, carry):
+            body(t)
+            return carry
+
+        lax.fori_loop(0, count, step, 0, unroll=4)
+
+    def go_right(c, b):
+        return send(
+            going.at[c, b], from_left.at[c, b], sum_send.at[c, b], left_recv.at[c, b], right
+        )
+
+    def go_left(c, b):
+        return send(
+            going.at[c, b], from_right.at[c, b], sum_send.at[c, b], right_recv.at[c, b], left
+        )
+
+    def sums(c):
+        swap(c).wait_recv()
+
+        def one(b, to_right):
+            def fill(t):
+                going[c, b, t] = local(c, b * band + t)
+
+            loop(band, fill)
+            inner_side = i > 0 if to_right else i < n - 1
+            arrived = from_left if to_right else from_right
+
+            @pl.when(inner_side)
+            def _():
+                (go_right if to_right else go_left)(c, b).wait_recv()
+
+                def add(t):
+                    going[c, b, t] += arrived[c, b, t]
+
+                loop(band, add)
+
+            (go_right if to_right else go_left)(c, b).start()
+
+        for far in range(n - 1):
+            b = n - 1 - far
+            pl.when(b > i)(functools.partial(one, b, True))
+            pl.when(far < i)(functools.partial(one, far, False))
+
+    def share_right(c, b):
+        part = band_res[c].at[pl.ds(pl.multiple_of(b * band, band), band)]
+        return send(part, part, out_right.at[c, b], res_recv.at[c, b], right)
+
+    def share_left(c, b):
+        part = band_res[c].at[pl.ds(pl.multiple_of(b * band, band), band)]
+        return send(part, part, out_left.at[c, b], res_recv.at[c, b], left)
+
+    def finish(c):
+        def start_total(t):
+            total[t] = local(c, i * band + t)
+
+        loop(band, start_total)
+
+        @pl.when(i > 0)
+        def _():
+            go_right(c, i).wait_recv()
+
+            def add(t):
+                total[t] += from_left[c, i, t]
+
+            loop(band, add)
+
+        @pl.when(i < n - 1)
+        def _():
+            go_left(c, i).wait_recv()
+
+            def add(t):
+                total[t] += from_right[c, i, t]
+
+            loop(band, add)
+
+        if c == 0:
+            for copy in aux:
+                copy.wait_recv()
+        for j in range(owned):
+            t = o * owned + j
+            weight = wts[mine(c), j : j + 1]
+            value = weight * (sino[j, mine(c), :].astype(jnp.float32) - total[t])
+            band_res[c][i * band + t] = value.astype(jnp.bfloat16)
+            t = (1 - o) * owned + j
+            rows_here = pl.ds(c * depth, depth)
+            weight = mate_wts[rows_here, j : j + 1]
+            value = weight * (mate_sino[j, rows_here, :].astype(jnp.float32) - total[t])
+            band_res[c][i * band + t] = value.astype(jnp.bfloat16)
+
+        @pl.when(i < n - 1)
+        def _():
+            share_right(c, i).start()
+
+        @pl.when(i > 0)
+        def _():
+            share_left(c, i).start()
+
+    def relay(c):
+        for d in range(1, n):
+
+            @pl.when(i - d >= 0)
+            def _():
+                share_right(c, i - d).wait_recv()
+
+                @pl.when(i < n - 1)
+                def _():
+                    share_right(c, i - d).start()
+
+            @pl.when(i + d <= n - 1)
+            def _():
+                share_left(c, i + d).wait_recv()
+
+                @pl.when(i > 0)
+                def _():
+                    share_left(c, i + d).start()
+
+    def give(c):
+        return send(picked[c], landed[c], pick_send.at[c], pick_recv.at[c], mate)
+
+    def pick(c):
+        def for_mate(k):
+            picked[c][k] = band_res[c][mate_idx[k]]
+
+        loop(slots, for_mate)
+        give(c).start()
+
+        def for_self(k):
+            out_ref[k, mine(c), :] = band_res[c][own_idx[k]]
+
+        loop(slots, for_self)
+
+    def collect(c):
+        give(c).wait_recv()
+
+        def copy_in(k):
+            out_ref[k, theirs(c), :] = landed[c][k]
+
+        loop(slots, copy_in)
+
+    for step in range(pieces + 3):
+        for lag, stage in enumerate((sums, finish, relay, pick)):
+            if 0 <= step - lag < pieces:
+                stage(step - lag)
+    for c in range(pieces):
+        collect(c)
+
+    for copy in aux:
+        copy.wait_send()
+    for c in range(pieces):
+        swap(c).wait_send()
+        give(c).wait_send()
+        for b in range(n):
+
+            @pl.when(b > i)
+            def _():
+                go_right(c, b).wait_send()
+
+            @pl.when(b < i)
+            def _():
+                go_left(c, b).wait_send()
+
+            @pl.when(jnp.logical_and(b <= i, i < n - 1))
+            def _():
+                share_right(c, b).wait_send()
+
+            @pl.when(jnp.logical_and(b >= i, i > 0))
+            def _():
+                share_left(c, b).wait_send()
+
+
+def paired_path(volume, projector, slot_ray, slot_pixel, sinogram, weight_index, weight_table):
+    n = lax.axis_size("inner")
+    slots, per_slot, rows, cols = projector.shape
+    patch_tiles, _, slices = volume.shape
+    owned = sinogram.shape[0]
+    band = 2 * owned
+    rays = n * band
+    pieces = rows // 2 // PIECE
+    depth = PIECE
+    order = jnp.arange(slots, dtype=jnp.int32)
+    first = jnp.min(
+        jnp.where(slot_ray[:, None] == slot_ray[None, :], order[None, :], slots), axis=1
+    )
+    cell = jnp.min(
+        jnp.where(
+            jnp.arange(rays, dtype=jnp.int32)[:, None] == slot_ray[None, :], order[None, :], slots
+        ),
+        axis=1,
+    )
+    own_idx = jnp.concatenate([slot_ray, cell])
+    mate_idx = lax.ppermute(own_idx, "outer", [(0, 1), (1, 0)])
+    classes = weight_table.shape[0]
+    lookup = weight_index.T[:, :, None] == jnp.arange(classes)[None, None, :]
+    weights = jnp.sum(
+        jnp.where(lookup, weight_table.astype(jnp.float32)[None, None, :], 0.0), axis=2
+    )
+    weights = jnp.pad(weights, ((0, 0), (0, -owned % 128)))
+    pixel = slot_pixel.reshape(-1)
+    block = 4
+    tile_spec = pl.BlockSpec((block, per_slot, rows, cols), lambda s, *_: (s, 0, 0, 0))
+    volume_spec = pl.BlockSpec(volume.shape, lambda s, *_: (0, 0, 0))
+    packed = pl.pallas_call(
+        forward_kernel,
+        out_shape=jax.ShapeDtypeStruct((slots + 1, rows, slices), jnp.float32),
+        grid_spec=pltpu.PrefetchScalarGridSpec(
+            num_scalar_prefetch=2,
+            grid=(slots // block,),
+            in_specs=[volume_spec, tile_spec],
+            out_specs=pl.BlockSpec((slots + 1, rows, slices), lambda s, *_: (0, 0, 0)),
+        ),
+    )(first, pixel, volume, projector)
+    f32, bf16 = jnp.float32, jnp.bfloat16
+    dma = pltpu.SemaphoreType.DMA
+    vmem = pl.BlockSpec(memory_space=pltpu.VMEM)
+    smem = pl.BlockSpec(memory_space=pltpu.SMEM)
+    scratch = (
+        [pltpu.VMEM((slots + 1, depth, slices), f32)] * pieces
+        + [pltpu.VMEM((pieces, n, band, depth, slices), f32)] * 3
+        + [pltpu.VMEM((band, depth, slices), f32)]
+        + [pltpu.VMEM((rays, depth, slices), bf16)] * pieces
+        + [pltpu.VMEM((slots, depth, slices), bf16)] * (2 * pieces)
+        + [pltpu.VMEM((owned, rows // 2, slices), bf16), pltpu.VMEM((rows // 2, 128), f32)]
+        + [dma((pieces,)), dma((pieces,)), dma((2,)), dma((2,))]
+        + [dma((pieces, n))] * 6
+        + [dma((pieces,)), dma((pieces,))]
+    )
+    slot_residual = pl.pallas_call(
+        functools.partial(exchange_kernel, n, pieces),
+        out_shape=jax.ShapeDtypeStruct((slots, rows, slices), bf16),
+        in_specs=[smem, smem, vmem, vmem, vmem],
+        out_specs=vmem,
+        scratch_shapes=scratch,
+        compiler_params=pltpu.CompilerParams(collective_id=0, has_side_effects=True),
+    )(own_idx, mate_idx, packed, sinogram, weights)
+    return pl.pallas_call(
+        backward_kernel,
+        out_shape=jax.ShapeDtypeStruct(volume.shape, f32),
+        grid_spec=pltpu.PrefetchScalarGridSpec(
+            num_scalar_prefetch=1,
+            grid=(slots // block,),
+            in_specs=[
+                volume_spec,
+                tile_spec,
+                pl.BlockSpec((block, rows, slices), lambda s, *_: (s, 0, 0)),
+            ],
+            out_specs=pl.BlockSpec(volume.shape, lambda s, *_: (0, 0, 0)),
+            scratch_shapes=[pltpu.VMEM((patch_tiles, cols, 2 * slices), f32)],
+        ),
+    )(pixel, volume, projector, slot_residual)
+
+
+def on_device(volume, projector, slot_ray, slot_pixel, sinogram, weight_index, weight_table):
+    inners = lax.axis_size("inner")
+    outers = lax.axis_size("outer")
+    capacity = 2 * projector.shape[0] // inners
+    dense = sinogram.shape[0] * outers <= capacity
+    path = paired_path if outers == 2 and dense else general_path
+    return path(volume, projector, slot_ray, slot_pixel, sinogram, weight_index, weight_table)
+
+
 def solution(mesh):
     in_specs = (
         P(("group", "inner", "outer"), None, "cuts"),

time: 268 us -> 120 us (0.45)
  waiting for transfers between devices: 154 us -> 0.01 us
  Pallas kernels: 0 us -> 109 us
  matrix products: 36.8 us -> 0 us
  local copies, waits for them, and re-layouts: 31 us -> 2.67 us
  between operations: 13.6 us -> 0.02 us
  starting transfers between devices: 16.1 us -> 2.97 us
  blocking collectives: 8.58 us -> 0 us
  other arithmetic: 7.14 us -> 4.38 us
    all_to_all x3 -> x0, waiting for transfers between devices: 135 us -> none  [the longest x1 91.7 us: on_device(): lax.all_to_all(outgoing.reshape(inners, capacity, tile_rows, slice_count)...]
    pallas_call x0 -> x3, Pallas kernels: none -> 109 us  [the longest x1 92.8 us: paired_path(): pl.pallas_call(functools.partial(exchange_kernel, n, pieces), out_shape=j...]
    dot_general x18 -> x0, matrix products: 36.8 us -> none  [the longest x4 13.9 us: on_device(): jnp.einsum('srp,spc->src', projector[:, column], pixels, preferred_elemen...]
    reduce_scatter x1 -> x0, waiting for transfers between devices: 19.4 us -> none  [on_device(): lax.psum_scatter(block_sums, 'outer', scatter_dimension=0, tiled=True)]
    all_to_all x3 -> x0, starting transfers between devices: 16.1 us -> none  [the longest x1 6.35 us: on_device(): lax.all_to_all(labels.reshape(inners, capacity), 'inner', split_axis=0, c...]
    dot_general x4 -> x0, local copies, waits for them, and re-layouts: 10.7 us -> none  [on_device(): jnp.einsum('srp,src->spc', projector[:, column], slot_residual, preferred...]
    all_gather x1 -> x0, blocking collectives: 8.58 us -> none  [on_device(): residual = lax.all_gather(own_residual, 'outer', axis=0, tiled=True)]
    scatter x2 -> x0, local copies, waits for them, and re-layouts: 6.07 us -> none  [the longest x1 5.4 us: on_device(): jnp.zeros((cell_count, tile_rows, slice_count), jnp.float32).at[position]]
  transfers between devices with their start and end apart: 4 -> 1, of which waited for: 3 -> 0; matrix products, arithmetic and copies ran while one was open for 13% -> 4% of each run, Pallas kernels for 0% -> 7%
where the time goes in v1:
time: 120 us; the launch traced here: 119 us
  Pallas kernels  109 us (91%)
  other arithmetic  4.38 us (4%)
  starting transfers between devices  2.97 us (2%)
  local copies, waits for them, and re-layouts  2.67 us (2%)
    pallas_call x1, Pallas kernels, paired_path(): pl.pallas_call(functools.partial(exchange_kernel, n, pieces), out_shape=j...  92.8 us
    pallas_call x1, Pallas kernels, paired_path(): pl.pallas_call(backward_kernel, out_shape=jax.ShapeDtypeStruct(volume.sha...  8.61 us
    pallas_call x1, Pallas kernels, paired_path(): pl.pallas_call(forward_kernel, out_shape=jax.ShapeDtypeStruct((slots + 1,...  8 us
    ppermute x1, starting transfers between devices, paired_path(): mate_idx = lax.ppermute(own_idx, 'outer', [(0, 1), (1, 0)])  2.97 us
  transfers between devices with their start and end apart: 1, of which 0 were waited for; matrix products, arithmetic and copies ran while one was open for 4% of the time, Pallas kernels for 7%

profile of v1, /device:TPU:0, one launch (start us, length us, event | category | flops | bytes accessed | tf_op | source)
XLA Modules:
  0.0 119.5 jit_solution(13449907433336704825)
XLA Ops:
  0.0 0.7 select_reduce_fusion.2
  0.7 0.7 pad_add_fusion.own_idx
  1.5 0.0 copy-start
  1.5 3.0 %collective-permute-start = (s32[96]{0:T(128)S(1)}, s32[96]{0:T(128)S(1)}, u32[]{:S(2)}, u32[]{:S(2)}) collective-permute-start(s32[96]{0:T(128)S(1)} %pad_add_fusion.own_idx), channel_id=1, source_target_pairs={{0,2},{2,0},{1,3},{3,1},{4,6},{6,4},{5,7},{7,5},{8,10},{10,8},{9,1... | collective-permute-start | bytes 1160 | tf_op jit(solution)/shard_map/ppermute | solution.py:414
  4.4 1.5 %select_reduce_fusion.1.first_ref = s32[32]{0:T(128)} fusion(s32[32]{0:T(128)} %param.9), kind=kLoop, calls=%fused_computation.2 | loop fusion | flops 3040 | bytes 256 | tf_op jit(solution)/shard_map/reduce_min | solution.py:404
  5.9 0.7 convert_element_type.5
  6.6 0.8 copy.12
  7.3 0.8 select_reduce_fusion
  8.1 0.6 reshape.7.pixel_ref
  8.7 0.1 copy.13
  8.8 0.6 pad.4.wts
  9.4 8.0 %shard_map.73.packed = f32[33,128,128]{2,1,0:T(8,128)} custom-call(s32[32]{0:T(128)} %select_reduce_fusion.1.first_ref, s32[128]{0:T(128)} %reshape.7.pixel_ref, bf16[6,128,128]{2,1,0:T(8,128)(2,1)} %volume_ref.3, bf16[32,4,128,128]{3,2,1,0:T(8,128)(2,1)} %projector_ref.3), custom_call_target="tpu_custom_call" | custom-call | tf_op jit(solution)/shard_map/pallas_call | solution.py:425
  17.4 0.0 collective-permute-done.mate_idx
  17.4 0.0 copy-done
  17.5 0.0 copy-start.1
  17.5 0.6 copy-done.1
  18.0 92.8 %shard_map.74.residual_ref = bf16[32,128,128]{2,1,0:T(8,128)(2,1)} custom-call(s32[96]{0:T(128)} %copy-done, s32[96]{0:T(128)} %copy-done.1, f32[33,128,128]{2,1,0:T(8,128)} %shard_map.73.packed, bf16[8,128,128]{2,1,0:T(8,128)(2,1)} %sino.1, f32[128,128]{1,0:T(8,128)} %pad.4.wts), custom_call_target="tpu_custom_call" | custom-call | tf_op jit(solution)/shard_map/pallas_call | solution.py:450
  110.8 8.6 %shard_map.75 = f32[6,128,128]{2,1,0:T(8,128)} custom-call(s32[128]{0:T(128)} %reshape.7.pixel_ref, bf16[6,128,128]{2,1,0:T(8,128)(2,1)} %volume_ref.3, bf16[32,4,128,128]{3,2,1,0:T(8,128)(2,1)} %projector_ref.3, bf16[32,128,128]{2,1,0:T(8,128)(2,1)} %shard_map.74.residual_ref), custom_call_target="tpu_custom_call" | custom-call | tf_op jit(solution)/shard_map/pallas_call | solution.py:458
Async XLA Ops:
  1.5 16.0 %copy-start = (s32[96]{0:T(128)}, s32[96]{0:T(128)S(1)}, u32[]{:S(2)}) copy-start(s32[96]{0:T(128)S(1)} %pad_add_fusion.own_idx) | copy-start | bytes 1156
  1.5 16.0 %collective-permute-start = (s32[96]{0:T(128)S(1)}, s32[96]{0:T(128)S(1)}, u32[]{:S(2)}, u32[]{:S(2)}) collective-permute-start(s32[96]{0:T(128)S(1)} %pad_add_fusion.own_idx), channel_id=1, source_target_pairs={{0,2},{2,0},{1,3},{3,1},{4,6},{6,4},{5,7},{7,5},{8,10},{10,8},{9,1... | collective-permute-start | bytes 1160 | tf_op jit(solution)/shard_map/ppermute | solution.py:414
  17.5 0.6 copy-start.1

commit v2 on v1

--- a/solution.py
+++ b/solution.py
@@ -9,6 +9,7 @@
 
 MESH = pl.DeviceIdType.MESH
 PIECE = 16
+LIMIT = 32000.0
 
 
 def general_path(volume, projector, slot_ray, slot_pixel, sinogram, weight_index, weight_table):
@@ -102,9 +103,24 @@
     return volume.astype(jnp.float32) + backward / column_sum[:, :, None]
 
 
-def forward_kernel(first_ref, pixel_ref, volume_ref, projector_ref, packed_ref):
+def exponent_of(largest):
+    top = jnp.max(largest, axis=0, keepdims=True)
+    exponent = jnp.ceil(jnp.log2(jnp.maximum(top, 1e-20) * (1.0 / LIMIT)))
+    return jnp.broadcast_to(exponent, largest.shape)
+
+
+def encode(value, inverse):
+    return jnp.round(value * inverse).astype(jnp.int32).astype(jnp.int16)
+
+
+def decode(coded):
+    return coded.astype(jnp.int32).astype(jnp.float32)
+
+
+def forward_kernel(first_ref, pixel_ref, volume_ref, projector_ref, coded_ref, packed_ref):
     step = pl.program_id(0)
     block, per_slot = projector_ref.shape[:2]
+    slots, rows, slices = packed_ref.shape
 
     @pl.when(step == 0)
     def _():
@@ -117,6 +133,21 @@
         )
         tiles = jnp.concatenate([projector_ref[j, g] for g in range(per_slot)], axis=1)
         packed_ref[first_ref[s]] += jnp.dot(tiles, pixels, preferred_element_type=jnp.float32)
+
+    @pl.when(step == pl.num_programs(0) - 1)
+    def _():
+        largest = jnp.zeros((PIECE, slices), jnp.float32)
+        for s in range(slots):
+            for r in range(0, rows, PIECE):
+                largest = jnp.maximum(largest, jnp.abs(packed_ref[s, r : r + PIECE]))
+        exponent = exponent_of(largest)
+        inverse = jnp.exp2(-exponent)
+        for s in range(slots):
+            for r in range(0, rows, PIECE):
+                coded_ref[s, r : r + PIECE] = encode(packed_ref[s, r : r + PIECE], inverse)
+        for r in range(0, rows, PIECE):
+            coded_ref[slots, r : r + PIECE] = jnp.zeros((PIECE, slices), jnp.int16)
+            coded_ref[slots + 1, r : r + PIECE] = exponent.astype(jnp.int32).astype(jnp.int16)
 
 
 def backward_kernel(pixel_ref, volume_ref, projector_ref, residual_ref, out_ref, acc_ref):
@@ -197,8 +228,8 @@
 
     def swap(c):
         return send(
-            packed.at[pl.ds(0, slots), theirs(c)],
-            mate_part[c].at[pl.ds(0, slots)],
+            packed.at[:, theirs(c)],
+            mate_part[c],
             x_send.at[c],
             x_recv.at[c],
             mate,
@@ -214,11 +245,17 @@
         if c == min(1, pieces - 1):
             for copy in aux:
                 copy.start()
-    for c in range(pieces):
-        mate_part[c][slots] = jnp.zeros((depth, slices), jnp.float32)
-
-    def local(c, r):
-        return packed[own_idx[slots + r], mine(c), :] + mate_part[c][mate_idx[slots + r]]
+    def local_scales(c):
+        return (
+            jnp.exp2(decode(packed[slots + 1, mine(c), :])),
+            jnp.exp2(decode(mate_part[c][slots + 1])),
+        )
+
+    def local(c, r, scales):
+        return (
+            decode(packed[own_idx[slots + r], mine(c), :]) * scales[0]
+            + decode(mate_part[c][mate_idx[slots + r]]) * scales[1]
+        )
 
     def loop(count, body):
         def step(t, carry):
@@ -241,8 +278,10 @@
         swap(c).wait_recv()
 
         def one(b, to_right):
+            scales = local_scales(c)
+
             def fill(t):
-                going[c, b, t] = local(c, b * band + t)
+                total[t] = local(c, b * band + t, scales)
 
             loop(band, fill)
             inner_side = i > 0 if to_right else i < n - 1
@@ -252,11 +291,26 @@
             def _():
                 (go_right if to_right else go_left)(c, b).wait_recv()
 
+                scale = jnp.exp2(decode(arrived[c, b, band]))
+
                 def add(t):
-                    going[c, b, t] += arrived[c, b, t]
+                    total[t] += decode(arrived[c, b, t]) * scale
 
                 loop(band, add)
 
+            def widest(t, largest):
+                return jnp.maximum(largest, jnp.abs(total[t]))
+
+            exponent = exponent_of(
+                lax.fori_loop(0, band, widest, jnp.zeros((depth, slices), jnp.float32), unroll=4)
+            )
+            inverse = jnp.exp2(-exponent)
+
+            def pack(t):
+                going[c, b, t] = encode(total[t], inverse)
+
+            loop(band, pack)
+            going[c, b, band] = exponent.astype(jnp.int32).astype(jnp.int16)
             (go_right if to_right else go_left)(c, b).start()
 
         for far in range(n - 1):
@@ -273,8 +327,10 @@
         return send(part, part, out_left.at[c, b], res_recv.at[c, b], left)
 
     def finish(c):
+        scales = local_scales(c)
+
         def start_total(t):
-            total[t] = local(c, i * band + t)
+            total[t] = local(c, i * band + t, scales)
 
         loop(band, start_total)
 
@@ -282,8 +338,10 @@
         def _():
             go_right(c, i).wait_recv()
 
+            scale = jnp.exp2(decode(from_left[c, i, band]))
+
             def add(t):
-                total[t] += from_left[c, i, t]
+                total[t] += decode(from_left[c, i, t]) * scale
 
             loop(band, add)
 
@@ -291,8 +349,10 @@
         def _():
             go_left(c, i).wait_recv()
 
+            scale = jnp.exp2(decode(from_right[c, i, band]))
+
             def add(t):
-                total[t] += from_right[c, i, t]
+                total[t] += decode(from_right[c, i, t]) * scale
 
             loop(band, add)
 
@@ -424,12 +484,13 @@
     volume_spec = pl.BlockSpec(volume.shape, lambda s, *_: (0, 0, 0))
     packed = pl.pallas_call(
         forward_kernel,
-        out_shape=jax.ShapeDtypeStruct((slots + 1, rows, slices), jnp.float32),
+        out_shape=jax.ShapeDtypeStruct((slots + 2, rows, slices), jnp.int16),
         grid_spec=pltpu.PrefetchScalarGridSpec(
             num_scalar_prefetch=2,
             grid=(slots // block,),
             in_specs=[volume_spec, tile_spec],
-            out_specs=pl.BlockSpec((slots + 1, rows, slices), lambda s, *_: (0, 0, 0)),
+            out_specs=pl.BlockSpec((slots + 2, rows, slices), lambda s, *_: (0, 0, 0)),
+            scratch_shapes=[pltpu.VMEM((slots, rows, slices), jnp.float32)],
         ),
     )(first, pixel, volume, projector)
     f32, bf16 = jnp.float32, jnp.bfloat16
@@ -437,8 +498,8 @@
     vmem = pl.BlockSpec(memory_space=pltpu.VMEM)
     smem = pl.BlockSpec(memory_space=pltpu.SMEM)
     scratch = (
-        [pltpu.VMEM((slots + 1, depth, slices), f32)] * pieces
-        + [pltpu.VMEM((pieces, n, band, depth, slices), f32)] * 3
+        [pltpu.VMEM((slots + 2, depth, slices), jnp.int16)] * pieces
+        + [pltpu.VMEM((pieces, n, band + 1, depth, slices), jnp.int16)] * 3
         + [pltpu.VMEM((band, depth, slices), f32)]
         + [pltpu.VMEM((rays, depth, slices), bf16)] * pieces
         + [pltpu.VMEM((slots, depth, slices), bf16)] * (2 * pieces)

time: 120 us -> 108 us (0.900)
  Pallas kernels: 109 us -> 98 us
    pallas_call x1, Pallas kernels: 92.8 us -> 81.2 us  [paired_path(): pl.pallas_call(functools.partial(exchange_kernel, n, pieces), out_shape=j...]
  transfers between devices with their start and end apart: 1 -> 1, of which waited for: 0 -> 0; matrix products, arithmetic and copies ran while one was open for 4% -> 5% of each run, Pallas kernels for 7% -> 8%
where the time goes in v2:
time: 108 us
  Pallas kernels  98 us (91%)
  other arithmetic  4.3 us (4%)
  starting transfers between devices  2.97 us (3%)
  local copies, waits for them, and re-layouts  2.68 us (2%)
    pallas_call x1, Pallas kernels, paired_path(): pl.pallas_call(functools.partial(exchange_kernel, n, pieces), out_shape=j...  81.2 us
    pallas_call x1, Pallas kernels, paired_path(): pl.pallas_call(backward_kernel, out_shape=jax.ShapeDtypeStruct(volume.sha...  8.61 us
    pallas_call x1, Pallas kernels, paired_path(): pl.pallas_call(forward_kernel, out_shape=jax.ShapeDtypeStruct((slots + 2,...  8.15 us
    ppermute x1, starting transfers between devices, paired_path(): mate_idx = lax.ppermute(own_idx, 'outer', [(0, 1), (1, 0)])  2.97 us
  transfers between devices with their start and end apart: 1, of which 0 were waited for; matrix products, arithmetic and copies ran while one was open for 5% of the time, Pallas kernels for 8%

profile of v2, /device:TPU:0, one launch (start us, length us, event | category | flops | bytes accessed | tf_op | source)
XLA Modules:
  0.0 107.9 jit_solution(17995114646206944510)
XLA Ops:
  0.0 0.7 select_reduce_fusion.2
  0.7 0.7 pad_add_fusion.own_idx
  1.5 0.0 copy-start
  1.5 3.0 %collective-permute-start = (s32[96]{0:T(128)S(1)}, s32[96]{0:T(128)S(1)}, u32[]{:S(2)}, u32[]{:S(2)}) collective-permute-start(s32[96]{0:T(128)S(1)} %pad_add_fusion.own_idx), channel_id=1, source_target_pairs={{0,2},{2,0},{1,3},{3,1},{4,6},{6,4},{5,7},{7,5},{8,10},{10,8},{9,1... | collective-permute-start | bytes 1160 | tf_op jit(solution)/shard_map/ppermute | solution.py:474
  4.4 1.4 %select_reduce_fusion.1.first_ref = s32[32]{0:T(128)} fusion(s32[32]{0:T(128)} %param.9), kind=kLoop, calls=%fused_computation.2 | loop fusion | flops 3040 | bytes 256 | tf_op jit(solution)/shard_map/reduce_min | solution.py:464
  5.8 0.7 convert_element_type.5
  6.5 0.8 copy.12
  7.3 0.8 select_reduce_fusion
  8.0 0.7 reshape.7.pixel_ref
  8.7 0.1 copy.13
  8.8 0.6 pad.4.wts
  9.4 8.2 %shard_map.73.packed = s16[34,128,128]{2,1,0:T(8,128)(2,1)} custom-call(s32[32]{0:T(128)} %select_reduce_fusion.1.first_ref, s32[128]{0:T(128)} %reshape.7.pixel_ref, bf16[6,128,128]{2,1,0:T(8,128)(2,1)} %volume_ref.3, bf16[32,4,128,128]{3,2,1,0:T(8,128)(2,1)} %projector_ref.3), custom_call_target="tpu_custom_call" | custom-call | tf_op jit(solution)/shard_map/pallas_call | solution.py:485
  17.6 0.0 collective-permute-done.mate_idx
  17.6 0.0 copy-done
  17.6 0.0 copy-start.1
  17.6 0.5 copy-done.1
  18.1 81.2 %shard_map.74.residual_ref = bf16[32,128,128]{2,1,0:T(8,128)(2,1)} custom-call(s32[96]{0:T(128)} %copy-done, s32[96]{0:T(128)} %copy-done.1, s16[34,128,128]{2,1,0:T(8,128)(2,1)} %shard_map.73.packed, bf16[8,128,128]{2,1,0:T(8,128)(2,1)} %sino.1, f32[128,128]{1,0:T(8,128)} %pad.4.wts), custom_call_target="tpu_custom_call" | custom-call | tf_op jit(solution)/shard_map/pallas_call | solution.py:511
  99.3 8.6 %shard_map.75 = f32[6,128,128]{2,1,0:T(8,128)} custom-call(s32[128]{0:T(128)} %reshape.7.pixel_ref, bf16[6,128,128]{2,1,0:T(8,128)(2,1)} %volume_ref.3, bf16[32,4,128,128]{3,2,1,0:T(8,128)(2,1)} %projector_ref.3, bf16[32,128,128]{2,1,0:T(8,128)(2,1)} %shard_map.74.residual_ref), custom_call_target="tpu_custom_call" | custom-call | tf_op jit(solution)/shard_map/pallas_call | solution.py:519
Async XLA Ops:
  1.5 16.1 %copy-start = (s32[96]{0:T(128)}, s32[96]{0:T(128)S(1)}, u32[]{:S(2)}) copy-start(s32[96]{0:T(128)S(1)} %pad_add_fusion.own_idx) | copy-start | bytes 1156
  1.5 16.1 %collective-permute-start = (s32[96]{0:T(128)S(1)}, s32[96]{0:T(128)S(1)}, u32[]{:S(2)}, u32[]{:S(2)}) collective-permute-start(s32[96]{0:T(128)S(1)} %pad_add_fusion.own_idx), channel_id=1, source_target_pairs={{0,2},{2,0},{1,3},{3,1},{4,6},{6,4},{5,7},{7,5},{8,10},{10,8},{9,1... | collective-permute-start | bytes 1160 | tf_op jit(solution)/shard_map/ppermute | solution.py:474
  17.6 0.5 copy-start.1

commit v3 on v2

--- a/solution.py
+++ b/solution.py
@@ -180,7 +180,7 @@
 def exchange_kernel(n, pieces, own_idx, mate_idx, packed, sino, wts, out_ref, *scratch):
     take = iter(scratch)
     mate_part = [next(take) for _ in range(pieces)]
-    from_left, from_right, going, total = (next(take) for _ in range(4))
+    from_left, from_right, going, dense = (next(take) for _ in range(4))
     band_res = [next(take) for _ in range(pieces)]
     picked = [next(take) for _ in range(pieces)]
     landed = [next(take) for _ in range(pieces)]
@@ -274,49 +274,60 @@
             going.at[c, b], from_right.at[c, b], sum_send.at[c, b], right_recv.at[c, b], left
         )
 
-    def sums(c):
+    def gather(c):
         swap(c).wait_recv()
-
-        def one(b, to_right):
-            scales = local_scales(c)
-
-            def fill(t):
-                total[t] = local(c, b * band + t, scales)
-
-            loop(band, fill)
-            inner_side = i > 0 if to_right else i < n - 1
-            arrived = from_left if to_right else from_right
-
-            @pl.when(inner_side)
-            def _():
-                (go_right if to_right else go_left)(c, b).wait_recv()
-
-                scale = jnp.exp2(decode(arrived[c, b, band]))
-
-                def add(t):
-                    total[t] += decode(arrived[c, b, t]) * scale
-
-                loop(band, add)
-
-            def widest(t, largest):
-                return jnp.maximum(largest, jnp.abs(total[t]))
-
-            exponent = exponent_of(
-                lax.fori_loop(0, band, widest, jnp.zeros((depth, slices), jnp.float32), unroll=4)
-            )
-            inverse = jnp.exp2(-exponent)
-
-            def pack(t):
-                going[c, b, t] = encode(total[t], inverse)
-
-            loop(band, pack)
-            going[c, b, band] = exponent.astype(jnp.int32).astype(jnp.int16)
-            (go_right if to_right else go_left)(c, b).start()
-
-        for far in range(n - 1):
-            b = n - 1 - far
-            pl.when(b > i)(functools.partial(one, b, True))
-            pl.when(far < i)(functools.partial(one, far, False))
+        scales = local_scales(c)
+
+        def fill(r):
+            dense[c, r] = local(c, r, scales)
+
+        loop(n * band, fill)
+
+    def hop(c, b, to_right):
+        copy = (go_right if to_right else go_left)(c, b)
+        arrived = from_left if to_right else from_right
+
+        def widest(t, largest):
+            return jnp.maximum(largest, jnp.abs(dense[c, b * band + t]))
+
+        @pl.when(i > 0 if to_right else i < n - 1)
+        def _():
+            copy.wait_recv()
+            scale = jnp.exp2(decode(arrived[c, b, band]))
+
+            def add(t):
+                dense[c, b * band + t] += decode(arrived[c, b, t]) * scale
+
+            loop(band, add)
+
+        exponent = exponent_of(
+            lax.fori_loop(0, band, widest, jnp.zeros((depth, slices), jnp.float32), unroll=4)
+        )
+        inverse = jnp.exp2(-exponent)
+
+        def pack(t):
+            going[c, b, t] = encode(dense[c, b * band + t], inverse)
+
+        loop(band, pack)
+        going[c, b, band] = exponent.astype(jnp.int32).astype(jnp.int16)
+        copy.start()
+
+    def sums(step):
+        def rightward(far, carry):
+            hop(step - i, n - 1 - far, True)
+            return carry
+
+        def leftward(far, carry):
+            hop(step - (n - 1 - i), far, False)
+            return carry
+
+        @pl.when(jnp.logical_and(step >= i, step - i < pieces))
+        def _():
+            lax.fori_loop(0, n - 1 - i, rightward, 0)
+
+        @pl.when(jnp.logical_and(step >= n - 1 - i, step - (n - 1 - i) < pieces))
+        def _():
+            lax.fori_loop(0, i, leftward, 0)
 
     def share_right(c, b):
         part = band_res[c].at[pl.ds(pl.multiple_of(b * band, band), band)]
@@ -327,13 +338,6 @@
         return send(part, part, out_left.at[c, b], res_recv.at[c, b], left)
 
     def finish(c):
-        scales = local_scales(c)
-
-        def start_total(t):
-            total[t] = local(c, i * band + t, scales)
-
-        loop(band, start_total)
-
         @pl.when(i > 0)
         def _():
             go_right(c, i).wait_recv()
@@ -341,7 +345,7 @@
             scale = jnp.exp2(decode(from_left[c, i, band]))
 
             def add(t):
-                total[t] += decode(from_left[c, i, t]) * scale
+                dense[c, i * band + t] += decode(from_left[c, i, t]) * scale
 
             loop(band, add)
 
@@ -352,7 +356,7 @@
             scale = jnp.exp2(decode(from_right[c, i, band]))
 
             def add(t):
-                total[t] += decode(from_right[c, i, t]) * scale
+                dense[c, i * band + t] += decode(from_right[c, i, t]) * scale
 
             loop(band, add)
 
@@ -362,12 +366,12 @@
         for j in range(owned):
             t = o * owned + j
             weight = wts[mine(c), j : j + 1]
-            value = weight * (sino[j, mine(c), :].astype(jnp.float32) - total[t])
+            value = weight * (sino[j, mine(c), :].astype(jnp.float32) - dense[c, i * band + t])
             band_res[c][i * band + t] = value.astype(jnp.bfloat16)
             t = (1 - o) * owned + j
             rows_here = pl.ds(c * depth, depth)
             weight = mate_wts[rows_here, j : j + 1]
-            value = weight * (mate_sino[j, rows_here, :].astype(jnp.float32) - total[t])
+            value = weight * (mate_sino[j, rows_here, :].astype(jnp.float32) - dense[c, i * band + t])
             band_res[c][i * band + t] = value.astype(jnp.bfloat16)
 
         @pl.when(i < n - 1)
@@ -378,24 +382,22 @@
         def _():
             share_left(c, i).start()
 
-    def relay(c):
-        for d in range(1, n):
-
-            @pl.when(i - d >= 0)
+    def relay(c, d):
+        @pl.when(i - d >= 0)
+        def _():
+            share_right(c, i - d).wait_recv()
+
+            @pl.when(i < n - 1)
             def _():
-                share_right(c, i - d).wait_recv()
-
-                @pl.when(i < n - 1)
-                def _():
-                    share_right(c, i - d).start()
-
-            @pl.when(i + d <= n - 1)
+                share_right(c, i - d).start()
+
+        @pl.when(i + d <= n - 1)
+        def _():
+            share_left(c, i + d).wait_recv()
+
+            @pl.when(i > 0)
             def _():
-                share_left(c, i + d).wait_recv()
-
-                @pl.when(i > 0)
-                def _():
-                    share_left(c, i + d).start()
+                share_left(c, i + d).start()
 
     def give(c):
         return send(picked[c], landed[c], pick_send.at[c], pick_recv.at[c], mate)
@@ -420,10 +422,20 @@
 
         loop(slots, copy_in)
 
-    for step in range(pieces + 3):
-        for lag, stage in enumerate((sums, finish, relay, pick)):
-            if 0 <= step - lag < pieces:
-                stage(step - lag)
+    for step in range(pieces + 2 * (n - 1)):
+        if step < pieces:
+            gather(step)
+        if step < pieces + n - 1:
+            sums(step)
+        for d in range(n):
+            c = step - (n - 1) - d
+            if 0 <= c < pieces:
+                if d == 0:
+                    finish(c)
+                else:
+                    relay(c, d)
+                if d == n - 1:
+                    pick(c)
     for c in range(pieces):
         collect(c)
 
@@ -500,7 +512,7 @@
     scratch = (
         [pltpu.VMEM((slots + 2, depth, slices), jnp.int16)] * pieces
         + [pltpu.VMEM((pieces, n, band + 1, depth, slices), jnp.int16)] * 3
-        + [pltpu.VMEM((band, depth, slices), f32)]
+        + [pltpu.VMEM((pieces, rays, depth, slices), f32)]
         + [pltpu.VMEM((rays, depth, slices), bf16)] * pieces
         + [pltpu.VMEM((slots, depth, slices), bf16)] * (2 * pieces)
         + [pltpu.VMEM((owned, rows // 2, slices), bf16), pltpu.VMEM((rows // 2, 128), f32)]

time: 108 us -> 80.5 us (0.75)
  Pallas kernels: 98 us -> 70.1 us
    pallas_call x1, Pallas kernels: 81.2 us -> 53.3 us  [paired_path(): pl.pallas_call(functools.partial(exchange_kernel, n, pieces), out_shape=j...]
  transfers between devices with their start and end apart: 1 -> 1, of which waited for: 0 -> 0; matrix products, arithmetic and copies ran while one was open for 5% -> 6% of each run, Pallas kernels for 8% -> 10%
where the time goes in v3:
time: 80.5 us; the launch traced here: 80 us
  Pallas kernels  70.1 us (87%)
  other arithmetic  4.3 us (5%)
  starting transfers between devices  2.97 us (4%)
  local copies, waits for them, and re-layouts  2.68 us (3%)
    pallas_call x1, Pallas kernels, paired_path(): pl.pallas_call(functools.partial(exchange_kernel, n, pieces), out_shape=j...  53.3 us
    pallas_call x1, Pallas kernels, paired_path(): pl.pallas_call(backward_kernel, out_shape=jax.ShapeDtypeStruct(volume.sha...  8.61 us
    pallas_call x1, Pallas kernels, paired_path(): pl.pallas_call(forward_kernel, out_shape=jax.ShapeDtypeStruct((slots + 2,...  8.15 us
    ppermute x1, starting transfers between devices, paired_path(): mate_idx = lax.ppermute(own_idx, 'outer', [(0, 1), (1, 0)])  2.97 us
  transfers between devices with their start and end apart: 1, of which 0 were waited for; matrix products, arithmetic and copies ran while one was open for 6% of the time, Pallas kernels for 10%

profile of v3, /device:TPU:0, one launch (start us, length us, event | category | flops | bytes accessed | tf_op | source)
XLA Modules:
  0.0 80.0 jit_solution(7032207277501988735)
XLA Ops:
  0.0 0.7 select_reduce_fusion.2
  0.7 0.7 pad_add_fusion.own_idx
  1.5 0.0 copy-start
  1.5 3.0 %collective-permute-start = (s32[96]{0:T(128)S(1)}, s32[96]{0:T(128)S(1)}, u32[]{:S(2)}, u32[]{:S(2)}) collective-permute-start(s32[96]{0:T(128)S(1)} %pad_add_fusion.own_idx), channel_id=1, source_target_pairs={{0,2},{2,0},{1,3},{3,1},{4,6},{6,4},{5,7},{7,5},{8,10},{10,8},{9,1... | collective-permute-start | bytes 1160 | tf_op jit(solution)/shard_map/ppermute | solution.py:486
  4.4 1.4 %select_reduce_fusion.1.first_ref = s32[32]{0:T(128)} fusion(s32[32]{0:T(128)} %param.9), kind=kLoop, calls=%fused_computation.2 | loop fusion | flops 3040 | bytes 256 | tf_op jit(solution)/shard_map/reduce_min | solution.py:476
  5.8 0.7 convert_element_type.5
  6.5 0.8 copy.12
  7.3 0.8 select_reduce_fusion
  8.0 0.7 reshape.7.pixel_ref
  8.7 0.1 copy.13
  8.8 0.6 pad.4.wts
  9.4 8.2 %shard_map.73.packed = s16[34,128,128]{2,1,0:T(8,128)(2,1)} custom-call(s32[32]{0:T(128)} %select_reduce_fusion.1.first_ref, s32[128]{0:T(128)} %reshape.7.pixel_ref, bf16[6,128,128]{2,1,0:T(8,128)(2,1)} %volume_ref.3, bf16[32,4,128,128]{3,2,1,0:T(8,128)(2,1)} %projector_ref.3), custom_call_target="tpu_custom_call" | custom-call | tf_op jit(solution)/shard_map/pallas_call | solution.py:497
  17.6 0.0 collective-permute-done.mate_idx
  17.6 0.0 copy-done
  17.6 0.0 copy-start.1
  17.6 0.5 copy-done.1
  18.1 53.3 %shard_map.74.residual_ref = bf16[32,128,128]{2,1,0:T(8,128)(2,1)} custom-call(s32[96]{0:T(128)} %copy-done, s32[96]{0:T(128)} %copy-done.1, s16[34,128,128]{2,1,0:T(8,128)(2,1)} %shard_map.73.packed, bf16[8,128,128]{2,1,0:T(8,128)(2,1)} %sino.1, f32[128,128]{1,0:T(8,128)} %pad.4.wts), custom_call_target="tpu_custom_call" | custom-call | tf_op jit(solution)/shard_map/pallas_call | solution.py:523
  71.4 8.6 %shard_map.75 = f32[6,128,128]{2,1,0:T(8,128)} custom-call(s32[128]{0:T(128)} %reshape.7.pixel_ref, bf16[6,128,128]{2,1,0:T(8,128)(2,1)} %volume_ref.3, bf16[32,4,128,128]{3,2,1,0:T(8,128)(2,1)} %projector_ref.3, bf16[32,128,128]{2,1,0:T(8,128)(2,1)} %shard_map.74.residual_ref), custom_call_target="tpu_custom_call" | custom-call | tf_op jit(solution)/shard_map/pallas_call | solution.py:531
Async XLA Ops:
  1.5 16.1 %copy-start = (s32[96]{0:T(128)}, s32[96]{0:T(128)S(1)}, u32[]{:S(2)}) copy-start(s32[96]{0:T(128)S(1)} %pad_add_fusion.own_idx) | copy-start | bytes 1156
  1.5 16.1 %collective-permute-start = (s32[96]{0:T(128)S(1)}, s32[96]{0:T(128)S(1)}, u32[]{:S(2)}, u32[]{:S(2)}) collective-permute-start(s32[96]{0:T(128)S(1)} %pad_add_fusion.own_idx), channel_id=1, source_target_pairs={{0,2},{2,0},{1,3},{3,1},{4,6},{6,4},{5,7},{7,5},{8,10},{10,8},{9,1... | collective-permute-start | bytes 1160 | tf_op jit(solution)/shard_map/ppermute | solution.py:486
  17.6 0.5 copy-start.1

commit v4 on v3

--- a/solution.py
+++ b/solution.py
@@ -117,22 +117,47 @@
     return coded.astype(jnp.int32).astype(jnp.float32)
 
 
-def forward_kernel(first_ref, pixel_ref, volume_ref, projector_ref, coded_ref, packed_ref):
+def forward_kernel(
+    ray_ref, pixel_ref, table_ref, index_ref, volume_ref, projector_ref, coded_ref, own_ref, wts_ref,
+    packed_ref,
+):
     step = pl.program_id(0)
     block, per_slot = projector_ref.shape[:2]
     slots, rows, slices = packed_ref.shape
+    rays = own_ref.shape[0] - slots
 
     @pl.when(step == 0)
     def _():
         packed_ref[...] = jnp.zeros_like(packed_ref)
 
+        def clear(r, carry):
+            own_ref[slots + r] = slots
+            return carry
+
+        lax.fori_loop(0, rays, clear, 0, unroll=8)
+
+        def enter(k, carry):
+            s = slots - 1 - k
+            own_ref[s] = ray_ref[s]
+            own_ref[slots + ray_ref[s]] = s
+            return carry
+
+        lax.fori_loop(0, slots, enter, 0, unroll=4)
+        index = index_ref[...]
+        weight = jnp.zeros(index.shape, jnp.float32)
+        for k in range(table_ref.shape[0]):
+            weight = jnp.where(index == k, table_ref[k], weight)
+        blank = jnp.zeros((rows - index.shape[0], rows), jnp.float32)
+        wts_ref[...] = jnp.concatenate([weight, blank], axis=0).T
+
     for j in range(block):
         s = step * block + j
         pixels = jnp.concatenate(
-            [volume_ref[pixel_ref[s * per_slot + g]] for g in range(per_slot)], axis=0
+            [volume_ref[pixel_ref[g, s]] for g in range(per_slot)], axis=0
         )
         tiles = jnp.concatenate([projector_ref[j, g] for g in range(per_slot)], axis=1)
-        packed_ref[first_ref[s]] += jnp.dot(tiles, pixels, preferred_element_type=jnp.float32)
+        cell = own_ref[slots + ray_ref[s]]
+        packed_ref[cell] += jnp.dot(tiles, pixels, preferred_element_type=jnp.float32)
 
     @pl.when(step == pl.num_programs(0) - 1)
     def _():
@@ -159,32 +184,30 @@
     def _():
         acc_ref[...] = jnp.zeros_like(acc_ref)
 
-    ones = jnp.ones((rows, slices), jnp.bfloat16)
+    ones = jnp.ones((PIECE, rows), jnp.bfloat16)
     for j in range(block):
         s = step * block + j
-        wide = jnp.concatenate([residual_ref[j], ones], axis=1)
+        tall = jnp.concatenate([residual_ref[j].T, ones], axis=0)
         tiles = jnp.concatenate([projector_ref[j, g] for g in range(per_slot)], axis=1)
-        spread = lax.dot_general(
-            tiles, wide, (((0,), (0,)), ((), ())), preferred_element_type=jnp.float32
-        )
+        spread = jnp.dot(tall, tiles, preferred_element_type=jnp.float32)
         for g in range(per_slot):
-            acc_ref[pixel_ref[s * per_slot + g]] += spread[g * cols : (g + 1) * cols]
+            acc_ref[pixel_ref[g, s]] += spread[:, g * cols : (g + 1) * cols]
 
     @pl.when(step == pl.num_programs(0) - 1)
     def _():
-        out_ref[...] = (
-            volume_ref[...].astype(jnp.float32) + acc_ref[:, :, :slices] / acc_ref[:, :, slices:]
-        )
-
-
-def exchange_kernel(n, pieces, own_idx, mate_idx, packed, sino, wts, out_ref, *scratch):
+        for q in range(acc_ref.shape[0]):
+            update = acc_ref[q, :slices] / acc_ref[q, slices : slices + 1]
+            out_ref[q] = volume_ref[q].astype(jnp.float32) + update.T
+
+
+def exchange_kernel(n, pieces, own_idx, packed, sino, wts, out_ref, *scratch):
     take = iter(scratch)
     mate_part = [next(take) for _ in range(pieces)]
     from_left, from_right, going, dense = (next(take) for _ in range(4))
     band_res = [next(take) for _ in range(pieces)]
     picked = [next(take) for _ in range(pieces)]
     landed = [next(take) for _ in range(pieces)]
-    mate_sino, mate_wts = next(take), next(take)
+    mate_sino, mate_wts, mate_idx = (next(take) for _ in range(3))
     x_send, x_recv, aux_send, aux_recv, sum_send, left_recv, right_recv = (
         next(take) for _ in range(7)
     )
@@ -240,6 +263,8 @@
         send(sino.at[:, other_half], mate_sino, aux_send.at[0], aux_recv.at[0], mate),
         send(wts.at[other_half], mate_wts, aux_send.at[1], aux_recv.at[1], mate),
     ]
+    table = send(own_idx, mate_idx, aux_send.at[2], aux_recv.at[2], mate)
+    table.start()
     for c in range(pieces):
         swap(c).start()
         if c == min(1, pieces - 1):
@@ -422,6 +447,7 @@
 
         loop(slots, copy_in)
 
+    table.wait_recv()
     for step in range(pieces + 2 * (n - 1)):
         if step < pieces:
             gather(step)
@@ -439,7 +465,7 @@
     for c in range(pieces):
         collect(c)
 
-    for copy in aux:
+    for copy in aux + [table]:
         copy.wait_send()
     for c in range(pieces):
         swap(c).wait_send()
@@ -472,39 +498,31 @@
     rays = n * band
     pieces = rows // 2 // PIECE
     depth = PIECE
-    order = jnp.arange(slots, dtype=jnp.int32)
-    first = jnp.min(
-        jnp.where(slot_ray[:, None] == slot_ray[None, :], order[None, :], slots), axis=1
-    )
-    cell = jnp.min(
-        jnp.where(
-            jnp.arange(rays, dtype=jnp.int32)[:, None] == slot_ray[None, :], order[None, :], slots
-        ),
-        axis=1,
-    )
-    own_idx = jnp.concatenate([slot_ray, cell])
-    mate_idx = lax.ppermute(own_idx, "outer", [(0, 1), (1, 0)])
-    classes = weight_table.shape[0]
-    lookup = weight_index.T[:, :, None] == jnp.arange(classes)[None, None, :]
-    weights = jnp.sum(
-        jnp.where(lookup, weight_table.astype(jnp.float32)[None, None, :], 0.0), axis=2
-    )
-    weights = jnp.pad(weights, ((0, 0), (0, -owned % 128)))
-    pixel = slot_pixel.reshape(-1)
-    block = 4
+    pixel = slot_pixel.T
+    block = 8
     tile_spec = pl.BlockSpec((block, per_slot, rows, cols), lambda s, *_: (s, 0, 0, 0))
     volume_spec = pl.BlockSpec(volume.shape, lambda s, *_: (0, 0, 0))
-    packed = pl.pallas_call(
+    whole = lambda shape: pl.BlockSpec(shape, lambda s, *_: (0,) * len(shape))
+    coded_shape = (slots + 2, rows, slices)
+    packed, own_idx, weights = pl.pallas_call(
         forward_kernel,
-        out_shape=jax.ShapeDtypeStruct((slots + 2, rows, slices), jnp.int16),
+        out_shape=(
+            jax.ShapeDtypeStruct(coded_shape, jnp.int16),
+            jax.ShapeDtypeStruct((slots + rays,), jnp.int32),
+            jax.ShapeDtypeStruct((rows, rows), jnp.float32),
+        ),
         grid_spec=pltpu.PrefetchScalarGridSpec(
-            num_scalar_prefetch=2,
+            num_scalar_prefetch=3,
             grid=(slots // block,),
-            in_specs=[volume_spec, tile_spec],
-            out_specs=pl.BlockSpec((slots + 2, rows, slices), lambda s, *_: (0, 0, 0)),
+            in_specs=[whole(weight_index.shape), volume_spec, tile_spec],
+            out_specs=(
+                whole(coded_shape),
+                pl.BlockSpec(memory_space=pltpu.SMEM),
+                whole((rows, rows)),
+            ),
             scratch_shapes=[pltpu.VMEM((slots, rows, slices), jnp.float32)],
         ),
-    )(first, pixel, volume, projector)
+    )(slot_ray, pixel, weight_table.astype(jnp.float32), weight_index, volume, projector)
     f32, bf16 = jnp.float32, jnp.bfloat16
     dma = pltpu.SemaphoreType.DMA
     vmem = pl.BlockSpec(memory_space=pltpu.VMEM)
@@ -516,18 +534,19 @@
         + [pltpu.VMEM((rays, depth, slices), bf16)] * pieces
         + [pltpu.VMEM((slots, depth, slices), bf16)] * (2 * pieces)
         + [pltpu.VMEM((owned, rows // 2, slices), bf16), pltpu.VMEM((rows // 2, 128), f32)]
-        + [dma((pieces,)), dma((pieces,)), dma((2,)), dma((2,))]
+        + [pltpu.SMEM((slots + rays,), jnp.int32)]
+        + [dma((pieces,)), dma((pieces,)), dma((3,)), dma((3,))]
         + [dma((pieces, n))] * 6
         + [dma((pieces,)), dma((pieces,))]
     )
     slot_residual = pl.pallas_call(
         functools.partial(exchange_kernel, n, pieces),
         out_shape=jax.ShapeDtypeStruct((slots, rows, slices), bf16),
-        in_specs=[smem, smem, vmem, vmem, vmem],
+        in_specs=[smem, vmem, vmem, vmem],
         out_specs=vmem,
         scratch_shapes=scratch,
         compiler_params=pltpu.CompilerParams(collective_id=0, has_side_effects=True),
-    )(own_idx, mate_idx, packed, sinogram, weights)
+    )(own_idx, packed, sinogram, weights)
     return pl.pallas_call(
         backward_kernel,
         out_shape=jax.ShapeDtypeStruct(volume.shape, f32),
@@ -540,7 +559,7 @@
                 pl.BlockSpec((block, rows, slices), lambda s, *_: (s, 0, 0)),
             ],
             out_specs=pl.BlockSpec(volume.shape, lambda s, *_: (0, 0, 0)),
-            scratch_shapes=[pltpu.VMEM((patch_tiles, cols, 2 * slices), f32)],
+            scratch_shapes=[pltpu.VMEM((patch_tiles, slices + PIECE, cols), f32)],
         ),
     )(pixel, volume, projector, slot_residual)
 

time: 80.5 us -> 69.8 us (0.87)
  other arithmetic: 4.3 us -> 1.23 us
  starting transfers between devices: 2.97 us -> 0 us
  local copies, waits for them, and re-layouts: 2.68 us -> 0 us
  Pallas kernels: 70.1 us -> 68.2 us
    ppermute x1 -> x0, starting transfers between devices: 2.97 us -> none  [paired_path(): mate_idx = lax.ppermute(own_idx, 'outer', [(0, 1), (1, 0)])]
    pallas_call x1, Pallas kernels: 8.61 us -> 5.92 us  [paired_path(): pl.pallas_call(backward_kernel, out_shape=jax.ShapeDtypeStruct(volume.sha...]
    pallas_call x1, Pallas kernels: 53.3 us -> 55.6 us  [paired_path(): pl.pallas_call(functools.partial(exchange_kernel, n, pieces), out_shape=j...]
    reduce_min x2 -> x0, other arithmetic: 2.14 us -> none  [the longest x1 1.4 us: paired_path(): jnp.min(jnp.where(slot_ray[:, None] == slot_ray[None, :], order[None, :],...]
    pallas_call x1, Pallas kernels: 8.15 us -> 6.66 us  [paired_path(): pl.pallas_call(forward_kernel, out_shape=(jax.ShapeDtypeStruct(coded_shap...]
    unnamed x5 -> x0, local copies, waits for them, and re-layouts: 1.27 us -> none
  transfers between devices with their start and end apart: 1 -> 0, of which waited for: 0 -> 0; matrix products, arithmetic and copies ran while one was open for 6% -> 0% of each run, Pallas kernels for 10% -> 0%
where the time goes in v4:
time: 69.8 us; the launch traced here: 69.5 us
  Pallas kernels  68.2 us (98%)
  other arithmetic  1.23 us (2%)
    pallas_call x1, Pallas kernels, paired_path(): pl.pallas_call(functools.partial(exchange_kernel, n, pieces), out_shape=j...  55.6 us
    pallas_call x1, Pallas kernels, paired_path(): pl.pallas_call(forward_kernel, out_shape=(jax.ShapeDtypeStruct(coded_shap...  6.66 us
    pallas_call x1, Pallas kernels, paired_path(): pl.pallas_call(backward_kernel, out_shape=jax.ShapeDtypeStruct(volume.sha...  5.92 us

profile of v4, /device:TPU:0, one launch (start us, length us, event | category | flops | bytes accessed | tf_op | source)
XLA Modules:
  0.0 69.5 jit_solution(652055212987912119)
XLA Ops:
  0.0 1.2 %convert_element_type.3.table_ref = f32[16]{0:T(128)} convert(bf16[16]{0:T(256)(128)(2,1)} %param.13) | non-fusion elementwise | flops 16 | bytes 96 | tf_op jit(solution)/shard_map/convert_element_type | solution.py:525
  1.2 6.7 %shard_map.73 = (s16[34,128,128]{2,1,0:T(8,128)(2,1)}, s32[96]{0:T(128)}, f32[128,128]{1,0:T(8,128)}) custom-call(s32[32]{0:T(128)} %ray_ref.1, s32[4,32]{1,0:T(4,128)} %bitcast.1, f32[16]{0:T(128)} %convert_element_type.3.table_ref, s32[8,128]{1,0:T(8,128)} %index_ref.1, bf16[6,128,128]{2,1,0:T(8,128)(2,1)} %volume_ref.3, ...), custom_call_target="tpu_custom_call" | custom-call | tf_op jit(solution)/shard_map/pallas_call | solution.py:507
  7.9 55.6 %shard_map.74.residual_ref = bf16[32,128,128]{2,1,0:T(8,128)(2,1)} custom-call(s32[96]{0:T(128)} %get-tuple-element.8.own_idx, s16[34,128,128]{2,1,0:T(8,128)(2,1)} %get-tuple-element.9.packed, bf16[8,128,128]{2,1,0:T(8,128)(2,1)} %sino.1, f32[128,128]{1,0:T(8,128)} %get-tuple-element.10.wts), custom_call_target="tpu_custom_call" | custom-call | tf_op jit(solution)/shard_map/pallas_call | solution.py:542
  63.5 5.9 %shard_map.75 = f32[6,128,128]{2,1,0:T(8,128)} custom-call(s32[4,32]{1,0:T(4,128)} %bitcast.2, bf16[6,128,128]{2,1,0:T(8,128)(2,1)} %volume_ref.3, bf16[32,4,128,128]{3,2,1,0:T(8,128)(2,1)} %projector_ref.3, bf16[32,128,128]{2,1,0:T(8,128)(2,1)} %shard_map.74.residual_ref), custom_call_target="tpu_custom_call" | custom-call | tf_op jit(solution)/shard_map/pallas_call | solution.py:550

commit v5 on v4

--- a/solution.py
+++ b/solution.py
@@ -118,7 +118,7 @@
 
 
 def forward_kernel(
-    ray_ref, pixel_ref, table_ref, index_ref, volume_ref, projector_ref, coded_ref, own_ref, wts_ref,
+    ray_ref, pixel_ref, index_ref, table_ref, volume_ref, projector_ref, coded_ref, own_ref, wts_ref,
     packed_ref,
 ):
     step = pl.program_id(0)
@@ -145,8 +145,9 @@
         lax.fori_loop(0, slots, enter, 0, unroll=4)
         index = index_ref[...]
         weight = jnp.zeros(index.shape, jnp.float32)
-        for k in range(table_ref.shape[0]):
-            weight = jnp.where(index == k, table_ref[k], weight)
+        table = table_ref[...].astype(jnp.float32)
+        for k in range(table.shape[1]):
+            weight = jnp.where(index == k, table[:, k : k + 1], weight)
         blank = jnp.zeros((rows - index.shape[0], rows), jnp.float32)
         wts_ref[...] = jnp.concatenate([weight, blank], axis=0).T
 
@@ -339,20 +340,17 @@
 
     def sums(step):
         def rightward(far, carry):
-            hop(step - i, n - 1 - far, True)
+            c = step - i - far
+            pl.when(jnp.logical_and(c >= 0, c < pieces))(lambda: hop(c, n - 1 - far, True))
             return carry
 
         def leftward(far, carry):
-            hop(step - (n - 1 - i), far, False)
+            c = step - (n - 1 - i) - far
+            pl.when(jnp.logical_and(c >= 0, c < pieces))(lambda: hop(c, far, False))
             return carry
 
-        @pl.when(jnp.logical_and(step >= i, step - i < pieces))
-        def _():
-            lax.fori_loop(0, n - 1 - i, rightward, 0)
-
-        @pl.when(jnp.logical_and(step >= n - 1 - i, step - (n - 1 - i) < pieces))
-        def _():
-            lax.fori_loop(0, i, leftward, 0)
+        lax.fori_loop(0, n - 1 - i, rightward, 0)
+        lax.fori_loop(0, i, leftward, 0)
 
     def share_right(c, b):
         part = band_res[c].at[pl.ds(pl.multiple_of(b * band, band), band)]
@@ -499,6 +497,7 @@
     pieces = rows // 2 // PIECE
     depth = PIECE
     pixel = slot_pixel.T
+    classes = weight_table.shape[0]
     block = 8
     tile_spec = pl.BlockSpec((block, per_slot, rows, cols), lambda s, *_: (s, 0, 0, 0))
     volume_spec = pl.BlockSpec(volume.shape, lambda s, *_: (0, 0, 0))
@@ -512,9 +511,9 @@
             jax.ShapeDtypeStruct((rows, rows), jnp.float32),
         ),
         grid_spec=pltpu.PrefetchScalarGridSpec(
-            num_scalar_prefetch=3,
+            num_scalar_prefetch=2,
             grid=(slots // block,),
-            in_specs=[whole(weight_index.shape), volume_spec, tile_spec],
+            in_specs=[whole(weight_index.shape), whole((1, classes)), volume_spec, tile_spec],
             out_specs=(
                 whole(coded_shape),
                 pl.BlockSpec(memory_space=pltpu.SMEM),
@@ -522,7 +521,7 @@
             ),
             scratch_shapes=[pltpu.VMEM((slots, rows, slices), jnp.float32)],
         ),
-    )(slot_ray, pixel, weight_table.astype(jnp.float32), weight_index, volume, projector)
+    )(slot_ray, pixel, weight_index, weight_table.reshape(1, classes), volume, projector)
     f32, bf16 = jnp.float32, jnp.bfloat16
     dma = pltpu.SemaphoreType.DMA
     vmem = pl.BlockSpec(memory_space=pltpu.VMEM)

time: 69.8 us -> 69 us (0.989)
  other arithmetic: 1.23 us -> 0 us
    convert_element_type x1 -> x0, other arithmetic: 1.23 us -> none  [paired_path(): weight_table.astype(jnp.float32)]
where the time goes in v5:
time: 69 us; the launch traced here: 68.7 us
  Pallas kernels  68.7 us (100%)
    pallas_call x1, Pallas kernels, paired_path(): pl.pallas_call(functools.partial(exchange_kernel, n, pieces), out_shape=j...  56 us
    pallas_call x1, Pallas kernels, paired_path(): pl.pallas_call(forward_kernel, out_shape=(jax.ShapeDtypeStruct(coded_shap...  6.79 us
    pallas_call x1, Pallas kernels, paired_path(): pl.pallas_call(backward_kernel, out_shape=jax.ShapeDtypeStruct(volume.sha...  5.92 us

profile of v5, /device:TPU:0, one launch (start us, length us, event | category | flops | bytes accessed | tf_op | source)
XLA Modules:
  0.0 68.7 jit_solution(1826650728563602129)
XLA Ops:
  0.0 6.8 %shard_map.73 = (s16[34,128,128]{2,1,0:T(8,128)(2,1)}, s32[96]{0:T(128)}, f32[128,128]{1,0:T(8,128)}) custom-call(s32[32]{0:T(128)} %ray_ref.1, s32[4,32]{1,0:T(4,128)} %bitcast.2, s32[8,128]{1,0:T(8,128)} %index_ref.1, bf16[1,16]{1,0:T(2,128)(2,1)} %bitcast.4, bf16[6,128,128]{2,1,0:T(8,128)(2,1)} %volume_ref.3, bf16[32,4,128,128]{3,2,1,0:T(8,128)(2,1)} %projector_ref.3), custom_call_target="tpu_custom_call" | custom-call | tf_op jit(solution)/shard_map/pallas_call | solution.py:506
  6.8 56.0 %shard_map.74.residual_ref = bf16[32,128,128]{2,1,0:T(8,128)(2,1)} custom-call(s32[96]{0:T(128)} %get-tuple-element.8.own_idx, s16[34,128,128]{2,1,0:T(8,128)(2,1)} %get-tuple-element.9.packed, bf16[8,128,128]{2,1,0:T(8,128)(2,1)} %sino.1, f32[128,128]{1,0:T(8,128)} %get-tuple-element.10.wts), custom_call_target="tpu_custom_call" | custom-call | tf_op jit(solution)/shard_map/pallas_call | solution.py:541
  62.8 5.9 %shard_map.75 = f32[6,128,128]{2,1,0:T(8,128)} custom-call(s32[4,32]{1,0:T(4,128)} %bitcast.3, bf16[6,128,128]{2,1,0:T(8,128)(2,1)} %volume_ref.3, bf16[32,4,128,128]{3,2,1,0:T(8,128)(2,1)} %projector_ref.3, bf16[32,128,128]{2,1,0:T(8,128)(2,1)} %shard_map.74.residual_ref), custom_call_target="tpu_custom_call" | custom-call | tf_op jit(solution)/shard_map/pallas_call | solution.py:549

commit v6 on v5

--- a/solution.py
+++ b/solution.py
@@ -268,7 +268,7 @@
     table.start()
     for c in range(pieces):
         swap(c).start()
-        if c == min(1, pieces - 1):
+        if c == pieces - 1:
             for copy in aux:
                 copy.start()
     def local_scales(c):

time: 69 us -> 66.3 us (0.961)
  Pallas kernels: 68.7 us -> 66 us
    pallas_call x1, Pallas kernels: 56 us -> 53.3 us  [paired_path(): pl.pallas_call(functools.partial(exchange_kernel, n, pieces), out_shape=j...]
where the time goes in v6:
time: 66.3 us; the launch traced here: 66 us
  Pallas kernels  66 us (100%)
    pallas_call x1, Pallas kernels, paired_path(): pl.pallas_call(functools.partial(exchange_kernel, n, pieces), out_shape=j...  53.3 us
    pallas_call x1, Pallas kernels, paired_path(): pl.pallas_call(forward_kernel, out_shape=(jax.ShapeDtypeStruct(coded_shap...  6.79 us
    pallas_call x1, Pallas kernels, paired_path(): pl.pallas_call(backward_kernel, out_shape=jax.ShapeDtypeStruct(volume.sha...  5.92 us

profile of v6, /device:TPU:0, one launch (start us, length us, event | category | flops | bytes accessed | tf_op | source)
XLA Modules:
  0.0 66.0 jit_solution(14675260264756384559)
XLA Ops:
  0.0 6.8 %shard_map.73 = (s16[34,128,128]{2,1,0:T(8,128)(2,1)}, s32[96]{0:T(128)}, f32[128,128]{1,0:T(8,128)}) custom-call(s32[32]{0:T(128)} %ray_ref.1, s32[4,32]{1,0:T(4,128)} %bitcast.2, s32[8,128]{1,0:T(8,128)} %index_ref.1, bf16[1,16]{1,0:T(2,128)(2,1)} %bitcast.4, bf16[6,128,128]{2,1,0:T(8,128)(2,1)} %volume_ref.3, bf16[32,4,128,128]{3,2,1,0:T(8,128)(2,1)} %projector_ref.3), custom_call_target="tpu_custom_call" | custom-call | tf_op jit(solution)/shard_map/pallas_call | solution.py:506
  6.8 53.3 %shard_map.74.residual_ref = bf16[32,128,128]{2,1,0:T(8,128)(2,1)} custom-call(s32[96]{0:T(128)} %get-tuple-element.8.own_idx, s16[34,128,128]{2,1,0:T(8,128)(2,1)} %get-tuple-element.9.packed, bf16[8,128,128]{2,1,0:T(8,128)(2,1)} %sino.1, f32[128,128]{1,0:T(8,128)} %get-tuple-element.10.wts), custom_call_target="tpu_custom_call" | custom-call | tf_op jit(solution)/shard_map/pallas_call | solution.py:541
  60.1 5.9 %shard_map.75 = f32[6,128,128]{2,1,0:T(8,128)} custom-call(s32[4,32]{1,0:T(4,128)} %bitcast.3, bf16[6,128,128]{2,1,0:T(8,128)(2,1)} %volume_ref.3, bf16[32,4,128,128]{3,2,1,0:T(8,128)(2,1)} %projector_ref.3, bf16[32,128,128]{2,1,0:T(8,128)(2,1)} %shard_map.74.residual_ref), custom_call_target="tpu_custom_call" | custom-call | tf_op jit(solution)/shard_map/pallas_call | solution.py:549
